TPU v7x, 512 devices: a whole 4x8x8 slice. The times are simulated.
512 devices in a mesh: tm: 32 (over x, z), space: 16 (over y, core).
Axes of the slice: x: 4, y: 8, z: 8, core: 2. Of those that a mesh axis runs over, the one named last changes fastest.
Arguments:
- inverse_factor: bfloat16 [32, 2048, 2048], P('tm', None, 'space'), as said below
- arrow_factor: bfloat16 [32, 64, 2048], P('tm', None, 'space'), may hold values from -6 to 6
- decay: float32 [32, 2048], P('tm'), may hold values from 0 to 1
- tip_inverse: float32 [64, 64], replicated, may hold values from -0.75 to 0.75
- sigma_end: float32 [2048, 2048], P(None, 'space'), may hold values from -2.7 to 2.7, as said below
- arrow_end: float32 [2048, 64], P('space'), may hold values from -6 to 6
Outputs:
- sigmas: float32 [32, 2048, 2048], P('tm', None, 'space')
- arrows: float32 [32, 2048, 64], P('tm', 'space')
Inputs may be any that keep to these rules, and one draw needn't show every extreme that they name: `inverse_factor`: each K_t is lower triangular with a positive diagonal. `sigma_end`: symmetric.
All inputs are finite; a program needn't handle non-finite values.
Results may differ from a plain program's by a relative error of at most 0.0003.
Values may be sent and summed in bfloat16 or wider, within the bound.
No kernel may reach another device: no remote copies, remote signals or barrier semaphores. Data moves between devices by JAX's collectives and lax.ppermute only.
A program may use at most 128 MiB of HBM per device.

v0:
```python
import jax
import jax.numpy as jnp
from jax import lax
from jax.sharding import PartitionSpec as P


def prefix(array, axis, combine, identity):
    devices, position = (lax.axis_size(axis), lax.axis_index(axis))
    everything = jax.tree.map(lambda part: lax.all_gather(part, axis), array)
    start = jax.tree.map(
        lambda part, zero: jnp.broadcast_to(jnp.asarray(zero, part.dtype), part.shape),
        array,
        identity,
    )

    def hop(k, before):
        at = devices - 1 - k
        reached = at > position
        new = combine(before, jax.tree.map(lambda part: part[at], everything))
        return jax.tree.map(lambda a, b: jnp.where(reached, a, b), new, before)

    return lax.fori_loop(0, devices, hop, start)


def column_products(left, right):
    return lax.dot_general(
        left, right, (((0,), (0,)), ((), ())), preferred_element_type=jnp.float32
    )


def compose(earlier, later):
    falloff_later, own_after, sigma_after, arrow_after = earlier
    lower_factor_current, own_here, sigma_here, border_column_current = later
    return (
        lower_factor_current * falloff_later,
        own_here * own_after,
        sigma_here + lower_factor_current[:, None] * own_here[None, :] * sigma_after,
        border_column_current + own_here[:, None] * arrow_after,
    )


def body(inverse_factor, arrow_factor, decay, tip_inverse, sigma_end, arrow_end):
    highest = lax.Precision.HIGHEST
    factor_cols = inverse_factor[0]
    order = factor_cols.shape[0]
    width = factor_cols.shape[1]
    panel_index = lax.axis_index("space")
    precision_panel = column_products(
        lax.all_gather(factor_cols, "space", axis=1, tiled=True), factor_cols
    )
    decay_all = decay[0]
    self_falloff = lax.dynamic_slice_in_dim(decay_all, panel_index * width, width)
    arrow_local = arrow_factor[0]
    arrow_wide = arrow_local.astype(jnp.float32)
    cross = lax.psum_scatter(
        lax.dot_general(
            precision_panel,
            arrow_wide,
            (((1,), (1,)), ((), ())),
            precision=highest,
            preferred_element_type=jnp.float32,
        ),
        "space",
        scatter_dimension=0,
        tiled=True,
    )
    own_arrow = -jnp.dot(cross, tip_inverse, precision=highest)
    arrow_cols_count = tip_inverse.shape[0]
    identity_matrix = (
        jnp.ones((order,), jnp.float32),
        jnp.ones((width,), jnp.float32),
        jnp.zeros((order, width), jnp.float32),
        jnp.zeros((width, arrow_cols_count), jnp.float32),
    )
    mine = (decay_all, self_falloff, precision_panel, own_arrow)
    later_decay, later_own, later_sigma, later_arrow = prefix(mine, "tm", compose, identity_matrix)
    covariance_following = later_sigma + later_decay[:, None] * later_own[None, :] * sigma_end
    spike_ahead = later_arrow + later_own[:, None] * arrow_end
    sigma_block = (
        precision_panel + decay_all[:, None] * self_falloff[None, :] * covariance_following
    )
    arrow_block = own_arrow + self_falloff[:, None] * spike_ahead
    return (sigma_block[None], arrow_block[None])


def solution(mesh):
    placed = (
        P("tm", None, "space"),
        P("tm", None, "space"),
        P("tm", None),
        P(),
        P(None, "space"),
        P("space", None),
    )
    return jax.shard_map(
        body,
        mesh=mesh,
        in_specs=placed,
        out_specs=(P("tm", None, "space"), P("tm", "space", None)),
        check_vma=False,
    )
```

profile of v0, /device:TPU:1, one launch (start us, length us, event | category | flops | bytes accessed | tf_op | source)
XLA Modules:
  0.0 611.4 jit_solution(3542080441122480926)
XLA Ops:
  8.0 76.7 %all-gather.9.cloned.1.call-done = bf16[1,2048,2048]{2,1,0:T(8,128)(2,1)} async-done(((bf16[1,2048,128]{2,1,0:T(8,128)(2,1)}), bf16[1,2048,2048]{2,1,0:T(8,128)(2,1)}) %all-gather.9.cloned.1.call-update) | async-done | bytes 8388624 | tf_op jit(solution)/shard_map/all_gather | solution.py:49
  84.7 5.8 fusion.3
  92.2 54.2 %reduce-scatter.2.cloned.1.call-done = f32[128,64]{1,0:T(8,128)} async-done(((f32[2048,64]{1,0:T(8,128)}), f32[128,64]{1,0:T(8,128)}) %reduce-scatter.2.cloned.1.call-update) | async-done | bytes 32784 | tf_op jit(solution)/shard_map/reduce_scatter | solution.py:55
  148.8 37.9 %all-gather.3 = f32[32,1,2048]{2,1,0:T(1,128)S(1)} all-gather(f32[1,1,2048]{2,1,0:T(1,128)S(1)} %bitcast.51), channel_id=1, replica_groups=mesh['tm'=32,'space'=16] {'tm'}, dimensions={0}, use_global_device_ids=true | all-gather | bytes 270336 | tf_op jit(solution)/shard_map/all_gather | solution.py:9
  187.4 33.0 %all-gather.4 = f32[32,1,128]{2,1,0:T(1,128)} all-gather(f32[1,1,128]{2,1,0:T(1,128)S(1)} %get-tuple-element.327), channel_id=1, replica_groups=mesh['tm'=32,'space'=16] {'tm'}, dimensions={0}, use_global_device_ids=true | all-gather | bytes 16896 | tf_op jit(solution)/shard_map/all_gather | solution.py:9
  220.4 4.0 all-gather.13.cloned.1.call-done
  224.4 3.1 copy.12
  227.5 243.0 %all-gather.11.cloned.1.call-done = f32[65536,128]{1,0:T(8,128)} async-done(((f32[2048,128]{1,0:T(8,128)}), f32[65536,128]{1,0:T(8,128)}) %all-gather.11.cloned.1.call-update) | async-done | bytes 33554448 | tf_op jit(solution)/shard_map/all_gather | solution.py:9
  470.5 130.7 %while.22 = (s32[]{:T(128)}, f32[2048]{0:T(1024)S(1)}, f32[128]{0:T(128)}, f32[2048,128]{1,0:T(8,128)S(1)}, f32[128,64]{1,0:T(8,128)S(1)}, /*index=5*/s32[]{:T(1...) while((s32[]{:T(128)}, f32[2048]{0:T(1024)S(1)}, ...), condition=%wide.region_2.3_spmd.clone, body=%wide.region_1.2_spmd.clone.sunk | while | flops 1350024 | bytes 3296485 | solution.py:22
  472.9 1.8 fusion.16
  477.0 1.8 fusion.16
  481.1 1.8 fusion.16
  485.2 1.8 fusion.16
  489.3 1.8 fusion.16
  493.3 1.8 fusion.16
  497.4 1.8 fusion.16
  501.5 1.8 fusion.16
  505.6 1.8 fusion.16
  509.7 1.8 fusion.16
  513.8 1.8 fusion.16
  517.8 1.8 fusion.16
  521.9 1.8 fusion.16
  526.0 1.8 fusion.16
  602.7 2.2 add_bitcast_fusion
  (178 shorter events, 111.0 us)
Async XLA Ops:
  7.2 139.2 %copy-start = (f32[64,64]{1,0:T(8,128)S(1)}, f32[64,64]{1,0:T(8,128)}, u32[]{:S(2)}) copy-start(f32[64,64]{1,0:T(8,128)} %param.11) | copy-start | bytes 49156
  7.2 83.3 %copy-start.6 = (bf16[1,64,128]{2,1,0:T(8,128)(2,1)S(1)}, bf16[1,64,128]{2,1,0:T(8,128)(2,1)}, u32[]{:S(2)}) copy-start(bf16[1,64,128]{2,1,0:T(8,128)(2,1)} %param.9) | copy-start | bytes 49156
  7.2 77.5 %all-gather.9.cloned.1.call-start = ((), (), s32[]{:S(2)}) async-start(), calls=%async_computation.2 | async-start | bytes 8912896 | tf_op jit(solution)/shard_map/all_gather | solution.py:49
  7.9 140.9 %copy-start.5 = (f32[1,2048]{1,0:T(1,128)S(1)}, f32[1,2048]{1,0:T(1,128)}, u32[]{:S(2)}) copy-start(f32[1,2048]{1,0:T(1,128)} %param.10) | copy-start | bytes 24580
  7.9 138.5 %reduce-scatter.2.cloned.1.call-start = ((), (), s32[]{:S(2)}) async-start(), calls=%async_computation.1 | async-start | bytes 1114112 | tf_op jit(solution)/shard_map/reduce_scatter | solution.py:55
  90.5 57.7 %copy-start.1 = (f32[2048,128]{1,0:T(8,128)}, f32[2048,128]{1,0:T(8,128)S(1)}, u32[]{:S(2)}) copy-start(f32[2048,128]{1,0:T(8,128)S(1)} %fusion.3) | copy-start | bytes 3145732
  92.1 132.3 %all-gather.13.cloned.1.call-start = ((), (), s32[]{:S(2)}) async-start(), calls=%async_computation.4 | async-start | bytes 1081344 | tf_op jit(solution)/shard_map/all_gather | solution.py:9
  148.1 322.3 %all-gather.11.cloned.1.call-start = ((), (), s32[]{:S(2)}) async-start(), calls=%async_computation.3 | async-start | bytes 34603008 | tf_op jit(solution)/shard_map/all_gather | solution.py:9
  470.5 130.8 %copy-start.4 = (f32[128,64]{0,1:T(8,128)S(1)}, f32[128,64]{0,1:T(8,128)}, u32[]{:S(2)}) copy-start(f32[128,64]{0,1:T(8,128)} %convolution_negate_fusion) | copy-start | bytes 98308
  470.5 132.2 %copy-start.2 = (f32[2048,128]{1,0:T(8,128)S(1)}, f32[2048,128]{1,0:T(8,128)}, u32[]{:S(2)}) copy-start(f32[2048,128]{1,0:T(8,128)} %copy-done.1) | copy-start | bytes 3145732
  470.5 132.2 %copy-start.3 = (f32[2048,128]{1,0:T(8,128)S(1)}, f32[2048,128]{1,0:T(8,128)}, u32[]{:S(2)}) copy-start(f32[2048,128]{1,0:T(8,128)} %param.12) | copy-start | bytes 3145732
Sparse Core Ops, SparseCore 0:
  10.1 74.5 all-gather.8
  92.2 54.1 reduce-scatter.1
  150.5 73.8 all-gather.12
  228.5 241.9 all-gather.10
where the time goes:
time: 615 us; the launch traced here: 611 us
  waiting for transfers between devices  379 us (62%)
  other arithmetic  132 us (21%)
  blocking collectives  70.9 us (12%)
  between operations  13.9 us (2%)
  matrix products  9.12 us (1%)
    all_gather x2, waiting for transfers between devices, prefix(): everything = jax.tree.map(lambda part: lax.all_gather(part, axis), array)  247 us
    select_n x128, other arithmetic, hop(): return jax.tree.map(lambda a, b: jnp.where(reached, a, b), new, before)  129 us
    all_gather x1, waiting for transfers between devices, body(): lax.all_gather(factor_cols, 'space', axis=1, tiled=True)  76.7 us
    all_gather x2, blocking collectives, prefix(): everything = jax.tree.map(lambda part: lax.all_gather(part, axis), array)  70.9 us
    reduce_scatter x1, waiting for transfers between devices, body(): lax.psum_scatter(lax.dot_general(precision_panel, arrow_wide, (((1,), (1,...  54.2 us
  transfers between devices with their start and end apart: 4, of which 4 were waited for; matrix products, arithmetic and copies ran while one was open for 1% of the time, Pallas kernels for 0%

commit v1 on v0

--- a/solution.py
+++ b/solution.py
@@ -46,7 +46,10 @@
     width = factor_cols.shape[1]
     panel_index = lax.axis_index("space")
     precision_panel = column_products(
-        lax.all_gather(factor_cols, "space", axis=1, tiled=True), factor_cols
+        jnp.concatenate(
+            lax.all_to_all(jnp.stack([factor_cols] * lax.axis_size("space")), "space", 0, 0), axis=1
+        ),
+        factor_cols,
     )
     decay_all = decay[0]
     self_falloff = lax.dynamic_slice_in_dim(decay_all, panel_index * width, width)

time: 615 us -> 734 us (1.19)
  blocking collectives: 70.9 us -> 266 us
  waiting for transfers between devices: 379 us -> 304 us
    all_to_all x0 -> x1, blocking collectives: none -> 195 us  [body(): lax.all_to_all(jnp.stack([factor_cols] * lax.axis_size('space')), 'space'...]
    all_gather x1 -> x0, waiting for transfers between devices: 76.7 us -> none  [body(): lax.all_gather(factor_cols, 'space', axis=1, tiled=True)]
  transfers between devices with their start and end apart: 4 -> 3, of which waited for: 4 -> 3; matrix products, arithmetic and copies ran while one was open for 1% -> 1% of each run, Pallas kernels for 0% -> 0%
where the time goes in v1:
time: 734 us; the launch traced here: 730 us
  waiting for transfers between devices  304 us (41%)
  blocking collectives  266 us (36%)
  other arithmetic  132 us (18%)
  between operations  13.9 us (2%)
    all_gather x2, waiting for transfers between devices, prefix(): everything = jax.tree.map(lambda part: lax.all_gather(part, axis), array)  247 us
    all_to_all x1, blocking collectives, body(): lax.all_to_all(jnp.stack([factor_cols] * lax.axis_size('space')), 'space'...  195 us
    select_n x128, other arithmetic, hop(): return jax.tree.map(lambda a, b: jnp.where(reached, a, b), new, before)  128 us
    all_gather x2, blocking collectives, prefix(): everything = jax.tree.map(lambda part: lax.all_gather(part, axis), array)  70.9 us
    reduce_scatter x1, waiting for transfers between devices, body(): lax.psum_scatter(lax.dot_general(precision_panel, arrow_wide, (((1,), (1,...  56 us
  transfers between devices with their start and end apart: 3, of which 3 were waited for; matrix products, arithmetic and copies ran while one was open for 1% of the time, Pallas kernels for 0%

profile of v1, /device:TPU:1, one launch (start us, length us, event | category | flops | bytes accessed | tf_op | source)
XLA Modules:
  0.0 729.7 jit_solution(772179466245330066)
XLA Ops:
  9.6 195.4 %all_to_all.5 = bf16[16,2048,128]{1,2,0:T(8,128)(2,1)S(1)} all-to-all(bf16[16,2048,128]{1,2,0:T(8,128)(2,1)S(1)} %stack.3), channel_id=1, replica_groups=mesh['tm'=32,'space'=16] {'space'}, dimensions={0} | all-to-all | bytes 16777216 | tf_op jit(solution)/shard_map/all_to_all | solution.py:50
  205.0 2.4 fusion.7
  209.0 56.0 %reduce-scatter.2.cloned.1.call-done = f32[128,64]{0,1:T(8,128)} async-done(((f32[2048,64]{0,1:T(8,128)}), f32[128,64]{0,1:T(8,128)}) %reduce-scatter.2.cloned.1.call-update) | async-done | bytes 32784 | tf_op jit(solution)/shard_map/reduce_scatter | solution.py:58
  267.4 37.8 %all-gather.2 = f32[32,1,2048]{2,1,0:T(1,128)S(1)} all-gather(f32[1,1,2048]{2,1,0:T(1,128)S(1)} %bitcast.54), channel_id=1, replica_groups=mesh['tm'=32,'space'=16] {'tm'}, dimensions={0}, use_global_device_ids=true | all-gather | bytes 270336 | tf_op jit(solution)/shard_map/all_gather | solution.py:9
  306.0 33.1 %all-gather.3 = f32[32,1,128]{2,1,0:T(1,128)} all-gather(f32[1,1,128]{2,1,0:T(1,128)S(1)} %get-tuple-element.337), channel_id=1, replica_groups=mesh['tm'=32,'space'=16] {'tm'}, dimensions={0}, use_global_device_ids=true | all-gather | bytes 16896 | tf_op jit(solution)/shard_map/all_gather | solution.py:9
  339.0 4.0 all-gather.9.cloned.1.call-done
  343.0 3.1 copy.16
  346.2 243.1 %all-gather.7.cloned.1.call-done = f32[65536,128]{1,0:T(8,128)} async-done(((f32[2048,128]{1,0:T(8,128)}), f32[65536,128]{1,0:T(8,128)}) %all-gather.7.cloned.1.call-update) | async-done | bytes 33554448 | tf_op jit(solution)/shard_map/all_gather | solution.py:9
  589.3 130.2 %while.22 = (s32[]{:T(128)}, f32[2048]{0:T(1024)S(1)}, f32[128]{0:T(128)}, f32[2048,128]{1,0:T(8,128)S(1)}, f32[128,64]{1,0:T(8,128)S(1)}, /*index=5*/s32[]{:T(1...) while((s32[]{:T(128)}, f32[2048]{0:T(1024)S(1)}, ...), condition=%wide.region_2.3_spmd.clone, body=%wide.region_1.2_spmd.clone.sunk | while | flops 1350024 | bytes 3296485 | solution.py:22
  591.7 1.8 fusion.16
  595.7 1.8 fusion.16
  599.8 1.8 fusion.16
  603.8 1.8 fusion.16
  607.9 1.8 fusion.16
  612.0 1.8 fusion.16
  616.0 1.8 fusion.16
  620.1 1.8 fusion.16
  624.1 1.8 fusion.16
  628.2 1.8 fusion.16
  632.3 1.8 fusion.16
  636.3 1.8 fusion.16
  640.4 1.8 fusion.16
  644.4 1.8 fusion.16
  721.0 2.2 add_bitcast_fusion
  (180 shorter events, 112.1 us)
Async XLA Ops:
  7.2 257.8 %copy-start = (f32[64,64]{1,0:T(8,128)S(1)}, f32[64,64]{1,0:T(8,128)}, u32[]{:S(2)}) copy-start(f32[64,64]{1,0:T(8,128)} %param.11) | copy-start | bytes 49156
  7.2 257.8 %reduce-scatter.2.cloned.1.call-start = ((), (), s32[]{:S(2)}) async-start(), calls=%async_computation.2 | async-start | bytes 557056 | tf_op jit(solution)/shard_map/reduce_scatter | solution.py:58
  9.5 195.4 %copy-start.4 = (bf16[1,2048,128]{2,1,0:T(8,128)(2,1)S(1)}, bf16[1,2048,128]{2,1,0:T(8,128)(2,1)}, u32[]{:S(2)}) copy-start(bf16[1,2048,128]{2,1,0:T(8,128)(2,1)} %param.8) | copy-start | bytes 1572868
  205.0 2.4 copy-start.7
  205.0 62.5 %copy-start.6 = (f32[1,2048]{1,0:T(1,128)S(1)}, f32[1,2048]{1,0:T(1,128)}, u32[]{:S(2)}) copy-start(f32[1,2048]{1,0:T(1,128)} %param.10) | copy-start | bytes 24580
  207.3 59.3 %copy-start.1 = (f32[2048,128]{1,0:T(8,128)}, f32[2048,128]{1,0:T(8,128)S(1)}, u32[]{:S(2)}) copy-start(f32[2048,128]{1,0:T(8,128)S(1)} %fusion.7) | copy-start | bytes 3145732
  208.9 134.1 %all-gather.9.cloned.1.call-start = ((), (), s32[]{:S(2)}) async-start(), calls=%async_computation.4 | async-start | bytes 1081344 | tf_op jit(solution)/shard_map/all_gather | solution.py:9
  266.6 322.6 %all-gather.7.cloned.1.call-start = ((), (), s32[]{:S(2)}) async-start(), calls=%async_computation.3 | async-start | bytes 34603008 | tf_op jit(solution)/shard_map/all_gather | solution.py:9
  589.3 130.3 %copy-start.5 = (f32[128,64]{0,1:T(8,128)S(1)}, f32[128,64]{0,1:T(8,128)}, u32[]{:S(2)}) copy-start(f32[128,64]{0,1:T(8,128)} %convolution_negate_fusion) | copy-start | bytes 98308
  589.3 131.7 %copy-start.2 = (f32[2048,128]{1,0:T(8,128)S(1)}, f32[2048,128]{1,0:T(8,128)}, u32[]{:S(2)}) copy-start(f32[2048,128]{1,0:T(8,128)} %copy-done.1) | copy-start | bytes 3145732
  589.3 131.7 %copy-start.3 = (f32[2048,128]{1,0:T(8,128)S(1)}, f32[2048,128]{1,0:T(8,128)}, u32[]{:S(2)}) copy-start(f32[2048,128]{1,0:T(8,128)} %param.12) | copy-start | bytes 3145732
Sparse Core Ops, SparseCore 0:
  209.0 55.9 reduce-scatter.1
  269.1 73.9 all-gather.8
  347.3 241.9 all-gather.6
